TPU v7x, 32 devices: a whole 2x2x4 slice. The times are simulated.
32 devices in a mesh: rows: 16 (over z, x, core), freq: 2 (over y).
Axes of the slice: x: 2, y: 2, z: 4, core: 2. Of those that a mesh axis runs over, the one named last changes fastest.
Arguments:
- design: float32 [128, 65536], P('rows'), may hold values from 0.05 to 0.95
- passive: int32 [128, 65536], P('rows'), may hold values 0 or 1
- state: bfloat16 [2, 2, 128, 65536], P(None, 'freq', 'rows'), may hold values from -36 to 36
- adjoint: bfloat16 [2, 2, 128, 65536], P(None, 'freq', 'rows'), may hold values from -36 to 36
- omega_sq: float32 [2], replicated, may hold values from 0.05 to 2
- assign: int32 [2], P('freq'), may hold values from 0 to 1, each once
Outputs:
- gradient: float32 [128, 65536], P('rows')
Inputs may be any that keep to these rules, and one draw needn't show every extreme that they name: `assign`: each of 0 .. 1 appears once.
All inputs are finite; a program needn't handle non-finite values. No bound on the sum of `passive` on one device may be relied on, other than what follows from the above.
Results may differ from a plain program's by a relative error of at most 0.0003.
Values may be sent and summed in bfloat16 or wider, within the bound.
A program may use at most 128 MiB of HBM per device.

v0:
```python
import jax
import jax.numpy as jnp
from jax import lax
from jax.sharding import PartitionSpec as P

RADIUS = 8


sharpness = 8.0
threshold = 0.5
exponent = 3.0
soft_floor = 0.001
loss_factor = 0.2
epsilon = 1e-06
stiff_table = [
    [4.0 / 6, -1.0 / 6, -1.0 / 6, -2.0 / 6],
    [-1.0 / 6, 4.0 / 6, -2.0 / 6, -1.0 / 6],
    [-1.0 / 6, -2.0 / 6, 4.0 / 6, -1.0 / 6],
    [-2.0 / 6, -1.0 / 6, -1.0 / 6, 4.0 / 6],
]
mass_table = [
    [4.0 / 36, 2.0 / 36, 2.0 / 36, 1.0 / 36],
    [2.0 / 36, 4.0 / 36, 1.0 / 36, 2.0 / 36],
    [2.0 / 36, 1.0 / 36, 4.0 / 36, 2.0 / 36],
    [1.0 / 36, 2.0 / 36, 2.0 / 36, 4.0 / 36],
]


def extended(block, sides, width):
    for axis, dim in sides:
        count = lax.axis_size(axis)
        forward = [(i, i + 1) for i in range(count - 1)]
        backward = [(target, source) for source, target in forward]
        low = lax.ppermute(
            lax.slice_in_dim(block, block.shape[dim] - width, None, axis=dim), axis, forward
        )
        high = lax.ppermute(lax.slice_in_dim(block, 0, width, axis=dim), axis, backward)
        block = jnp.concatenate([low, block, high], axis=dim)
    return block


def from_behind(block, axis, distance):
    devices = range(lax.axis_size(axis))
    route = [(i - distance, i) for i in devices if i - distance in devices]
    return lax.ppermute(block, axis, route)


def tap_list():
    return [float(RADIUS + 1 - abs(offset)) for offset in range(-RADIUS, RADIUS + 1)]


def row_pass(padded, count):
    taps = tap_list()
    total = taps[0] * padded[0:count]
    for offset in range(1, 2 * RADIUS + 1):
        total = total + taps[offset] * padded[offset : offset + count]
    return total


def col_pass(field):
    taps = tap_list()
    count = field.shape[1]
    padded = jnp.pad(field, ((0, 0), (RADIUS, RADIUS)))
    total = taps[0] * padded[:, 0:count]
    for offset in range(1, 2 * RADIUS + 1):
        total = total + taps[offset] * padded[:, offset : offset + count]
    return total


def edge_sums(start, count, whole):
    positions = start + jnp.arange(count, dtype=jnp.int32)
    total = jnp.zeros((count,), jnp.float32)
    for offset in range(-RADIUS, RADIUS + 1):
        inside = ((positions + offset >= 0) & (positions + offset < whole)).astype(jnp.float32)
        total = total + float(RADIUS + 1 - abs(offset)) * inside
    return total


def project(tilde, passive):
    bottom = jnp.tanh(sharpness * threshold) + jnp.tanh(sharpness * (1.0 - threshold))
    steep = jnp.tanh(sharpness * (tilde - threshold))
    value = (jnp.tanh(sharpness * threshold) + steep) / bottom
    slope = sharpness * (1.0 - steep * steep) / bottom
    solid = passive > 0
    density = jnp.where(solid, 1.0, value)
    slope = jnp.where(solid, 0.0, slope)
    stiffness = exponent * density * density * (1.0 - soft_floor)
    return (stiffness, slope)


def bilinear(table, left, right):
    total = None
    for row_pos in range(4):
        inner = table[row_pos][0] * right[0]
        for col_pos in range(1, 4):
            inner = inner + table[row_pos][col_pos] * right[col_pos]
        term = left[row_pos] * inner
        total = term if total is None else total + term
    return total


def corners(nodes, below):
    stacked = jnp.concatenate([nodes, below], axis=0)
    right_col = jnp.zeros((stacked.shape[0], 1), stacked.dtype)
    shifted = jnp.concatenate([stacked[:, 1:], right_col], axis=1)
    return (stacked[:-1], shifted[:-1], stacked[1:], shifted[1:])


def element_terms(fields, fields_below, duals, duals_below, stiffness, omega):
    state_real = corners(fields[0], fields_below[0])
    state_imag = corners(fields[1], fields_below[1])
    adjoint_real = corners(duals[0], duals_below[0])
    adjoint_imag = corners(duals[1], duals_below[1])
    elastic = bilinear(stiff_table, adjoint_real, state_real) - bilinear(
        stiff_table, adjoint_imag, state_imag
    )
    damped = bilinear(stiff_table, adjoint_real, state_imag) + bilinear(
        stiff_table, adjoint_imag, state_real
    )
    inertia = bilinear(mass_table, adjoint_real, state_real) - bilinear(
        mass_table, adjoint_imag, state_imag
    )
    return stiffness * (elastic - loss_factor * damped) - omega * inertia


def shards(design, passive, state, adjoint, omega_sq, assign):
    slab_rows, width = design.shape
    whole_rows = slab_rows * lax.axis_size("rows")
    top = lax.axis_index("rows") * slab_rows
    weight_sum = (
        edge_sums(top, slab_rows, whole_rows)[:, None] * edge_sums(0, width, width)[None, :]
    )
    padded = extended(design, (("rows", 0),), RADIUS)
    tilde = col_pass(row_pass(padded, slab_rows)) / weight_sum
    stiffness, slope = project(tilde, passive)
    factor = slope / weight_sum
    below_state, below_adjoint = from_behind((state[:, :, :1, :], adjoint[:, :, :1, :]), "rows", -1)
    table = jnp.arange(omega_sq.shape[0], dtype=jnp.int32)
    picked = (assign[:, None] == table[None, :]).astype(jnp.float32)
    omegas = jnp.sum(picked * omega_sq[None, :], axis=1)

    def accumulate(slot, total):
        fields = lax.dynamic_index_in_dim(state, slot, 1, keepdims=False).astype(jnp.float32)
        duals = lax.dynamic_index_in_dim(adjoint, slot, 1, keepdims=False).astype(jnp.float32)
        fields_below = lax.dynamic_index_in_dim(below_state, slot, 1, keepdims=False).astype(
            jnp.float32
        )
        duals_below = lax.dynamic_index_in_dim(below_adjoint, slot, 1, keepdims=False).astype(
            jnp.float32
        )
        omega = lax.dynamic_index_in_dim(omegas, slot, 0, keepdims=False)
        return total + element_terms(fields, fields_below, duals, duals_below, stiffness, omega)

    local = lax.fori_loop(0, state.shape[1], accumulate, jnp.zeros((slab_rows, width), jnp.float32))
    share = lax.psum_scatter(local, "freq", scatter_dimension=1, tiled=True)
    piece_cols = share.shape[1]
    start = lax.axis_index("freq") * piece_cols
    spread = share * lax.dynamic_slice_in_dim(factor, start, piece_cols, 1)
    padded_back = extended(spread, (("rows", 0),), RADIUS)
    rowed = row_pass(padded_back, slab_rows)
    joined = lax.all_gather(rowed, "freq", axis=1, tiled=True)
    back = col_pass(joined)
    total = lax.psum(jnp.sum(back * back), "rows")
    return back * lax.rsqrt(total / (whole_rows * width) + epsilon)


def solution(mesh):
    return jax.shard_map(
        shards,
        mesh=mesh,
        in_specs=(
            P("rows", None),
            P("rows", None),
            P(None, "freq", "rows", None),
            P(None, "freq", "rows", None),
            P(),
            P("freq"),
        ),
        out_specs=P("rows", None),
        check_vma=False,
    )
```

profile of v0, /device:TPU:0, one launch (start us, length us, event | category | flops | bytes accessed | tf_op | source)
XLA Modules:
  0.0 300.1 jit_solution(13670841534242166203)
XLA Ops:
  6.5 0.0 copy-start.4
  6.5 0.0 reduce-scatter.2.cloned.1.call-start
  6.5 3.9 %collective-permute-start = (f32[8,65536]{1,0:T(8,128)}, f32[8,65536]{1,0:T(8,128)}, u32[]{:S(2)}, u32[]{:S(2)}) collective-permute-start(f32[8,65536]{1,0:T(8,128)} %param.6), channel_id=1, source_target_pairs={{0,2},{2,4},{4,6},{6,8},{8,10},{10,12},{12,14},{14,16},{16,18},{18... | collective-permute-start | bytes 6291464 | tf_op jit(solution)/shard_map/ppermute | solution.py:34
  10.4 1.3 collective-permute-start.1
  11.7 1.9 slice.352
  13.6 0.4 copy.9
  14.0 1.3 collective-permute-start.2
  15.3 1.9 slice.358
  17.2 1.1 copy.10
  18.3 0.0 copy-start.5
  18.3 1.4 collective-permute-start.3
  19.7 0.0 copy-done.4
  19.7 0.3 convert_element_type.103
  20.0 0.0 copy-done.5
  20.0 0.3 convert_element_type.102
  20.3 1.6 slice_bitcast_fusion.2
  21.9 0.0 copy-start.9
  21.9 2.2 slice_bitcast_fusion.3
  24.8 0.0 copy-start.1
  24.8 0.0 copy-done.9
  24.8 0.6 fusion.172
  25.4 0.0 collective-permute-done.2
  25.4 0.2 convert_element_type.104
  25.6 0.4 slice_bitcast_fusion.7
  26.0 0.0 collective-permute-done.3
  26.0 1.1 convert_element_type.105
  27.1 0.4 slice_bitcast_fusion.6
  27.6 0.0 copy-start.6
  27.6 0.0 copy-start.7
  27.6 0.0 copy-done.1
  27.6 0.0 copy-start
  27.6 6.6 %slice_maximum_fusion = (f32[9,65535]{1,0:T(8,128)}, f32[9,65535]{1,0:T(8,128)}) fusion(f32[1,65536]{1,0:T(1,128)S(1)} %get-tuple-element.46, f32[8,65536]{1,0:T(8,128)} %get-tuple-element.36, f32[1,65536]{1,0:T(1,128)S(1)} %get-tuple-element.45, f32[8,65536]{1,0:T(8,128)S(1)} %copy-done.1), kind=kLoop, calls=%fused_computation | loop fusion | flops 1179630 | bytes 9437112 | tf_op jit(solution)/shard_map/while/body/eval_jaxpr/concatenate | solution.py:103
  34.2 0.0 copy-done.6
  34.2 0.0 copy-done.7
  34.2 0.0 copy-done
  34.2 4.9 %slice_maximum_fusion.1 = (f32[9,65535]{1,0:T(8,128)}, f32[9,65535]{1,0:T(8,128)}) fusion(f32[1,65536]{1,0:T(1,128)S(1)} %get-tuple-element.44, f32[8,65536]{1,0:T(8,128)S(1)} %copy-done, f32[1,65536]{1,0:T(1,128)S(1)} %get-tuple-element.43, f32[8,65536]{1,0:T(8,128)S(1)} %get-tuple-element.38), kind=kLoop, calls=%fused_computation.1 | loop fusion | flops 1179630 | bytes 9437112 | tf_op jit(solution)/shard_map/while/body/eval_jaxpr/concatenate | solution.py:103
  39.1 0.0 copy-start.2
  39.1 0.0 collective-permute-done
  39.1 1.9 constant_dynamic-update-slice_fusion.1
  41.0 0.3 copy-done.2
  41.3 0.3 constant_dynamic-update-slice_fusion
  41.6 0.0 collective-permute-done.1
  41.6 1.7 constant_dynamic-update-slice_fusion.2
  43.3 6.9 %fusion.4 = f32[8,65536]{1,0:T(8,128)} fusion(f32[8,65536]{1,0:T(8,128)} %collective-permute-done.1, f32[16,65536]{1,0:T(8,128)S(1)} %constant_dynamic-update-slice_fusion.2, f32[16,65536]{1,0:T(8,128)S(1)} %get-tuple-element.41, f32[8,65536]{1,0:T(8,128)} %collective-permute-done, f32[8,65536]{1,0:T(8,128)} %param.6), kind=kLoop, calls=%fused_computation.67 | loop fusion | flops 16252928 | bytes 37748736 | tf_op jit(solution)/shard_map/add | solution.py:56
  50.2 46.0 %fusion.2 = (f32[8,65536]{1,0:T(8,128)}, f32[8,65536]{1,0:T(8,128)}, pred[8,65536]{1,0:T(8,128)(4,1)}) fusion(f32[8,65536]{1,0:T(8,128)} %get-tuple-element.40, f32[8,65536]{1,0:T(8,128)} %get-tuple-element.36, f32[8,65536]{1,0:T(8,128)S(1)} %get-tuple-element.38, f32[8,65536]{1,0:T(8,128)} %get-tuple-element.26, f32[1,65536]{1,0:T(1,128)} %copy-done.7, ...), kind=kLoop, calls=%fused_computation.56 | loop fusion | flops 100663296 | bytes 28049300 | tf_op jit(solution)/shard_map/while/body/eval_jaxpr/sub | solution.py:123
  96.2 0.0 copy-start.3
  96.2 0.0 copy-start.8
  96.2 0.0 reduce-scatter.2.cloned.1.call-update
  96.2 0.0 all-gather.2.cloned.1.call-start
  96.3 1.5 broadcast_multiply_fusion.1
  97.8 69.1 %reduce-scatter.2.cloned.1.call-done = f32[8,32768]{1,0:T(8,128)} async-done(((f32[8,65536]{1,0:T(8,128)}), f32[8,32768]{1,0:T(8,128)}) %reduce-scatter.2.cloned.1.call-update) | async-done | bytes 1048592 | tf_op jit(solution)/shard_map/reduce_scatter | solution.py:155
  166.9 0.0 copy-done.3
  166.9 0.0 copy-done.8
  166.9 1.9 fusion.104
  168.7 1.3 collective-permute-start.5
  170.0 3.1 %collective-permute-start.4 = (f32[8,32768]{1,0:T(8,128)S(1)}, f32[8,32768]{1,0:T(8,128)S(1)}, u32[]{:S(2)}, u32[]{:S(2)}) collective-permute-start(f32[8,32768]{1,0:T(8,128)S(1)} %fusion.104), channel_id=1, source_target_pairs={{0,2},{2,4},{4,6},{6,8},{8,10},{10,12},{12,14},{14,16},{16,18},{18... | collective-permute-start | bytes 3145736 | tf_op jit(solution)/shard_map/ppermute | solution.py:34
  173.1 0.1 collective-permute-done.5
  173.3 2.1 collective-permute-done.4
  175.3 4.2 %fusion.66 = f32[8,32768]{1,0:T(8,128)} fusion(f32[8,32768]{1,0:T(8,128)S(1)} %collective-permute-done.5, f32[8,32768]{1,0:T(8,128)S(1)} %fusion.104, f32[8,32768]{1,0:T(8,128)S(1)} %collective-permute-done.4), kind=kLoop, calls=%fused_computation.159 | loop fusion | flops 11796480 | bytes 4194304 | tf_op jit(solution)/shard_map/add | solution.py:56
  179.6 0.0 all-gather.2.cloned.1.call-update
  179.6 53.8 %all-gather.2.cloned.1.call-done = f32[8,65536]{1,0:T(8,128)} async-done(((f32[8,32768]{1,0:T(8,128)}), f32[8,65536]{1,0:T(8,128)}) %all-gather.2.cloned.1.call-update) | async-done | bytes 2097168 | tf_op jit(solution)/shard_map/all_gather | solution.py:161
  233.4 24.1 %multiply_reduce_fusion = (f32[]{:T(128)}, f32[8,65536]{1,0:T(8,128)S(1)}) fusion(f32[8,65536]{1,0:T(8,128)} %all-gather.2.cloned.1.call-done), kind=kLoop, calls=%fused_computation.95 | loop fusion | flops 17301504 | bytes 4194308 | tf_op jit(solution)/shard_map/reduce_sum | solution.py:163
  257.5 33.6 %psum.7 = f32[]{:T(128)} all-reduce(f32[]{:T(128)} %get-tuple-element.21), channel_id=1, replica_groups=mesh['rows'=16,'freq'=2] {'rows'}, use_global_device_ids=true, to_apply=%region_3.4 | all-reduce | flops 1 | bytes 8 | tf_op jit(solution)/shard_map/psum | solution.py:163
  291.8 1.5 broadcast_multiply_fusion
  (2 shorter events, 0.0 us)
Async XLA Ops:
  6.5 13.2 %copy-start.4 = (bf16[2,1,8,65536]{3,2,1,0:T(8,128)(2,1)S(1)}, bf16[2,1,8,65536]{3,2,1,0:T(8,128)(2,1)}, u32[]{:S(2)}) copy-start(bf16[2,1,8,65536]{3,2,1,0:T(8,128)(2,1)} %param.8) | copy-start | bytes 6291460
  6.5 160.3 %reduce-scatter.2.cloned.1.call-start = ((), (), s32[]{:S(2)}) async-start(), calls=%async_computation.1 | async-start | bytes 3145728 | tf_op jit(solution)/shard_map/reduce_scatter | solution.py:155
  6.5 32.5 %collective-permute-start = (f32[8,65536]{1,0:T(8,128)}, f32[8,65536]{1,0:T(8,128)}, u32[]{:S(2)}, u32[]{:S(2)}) collective-permute-start(f32[8,65536]{1,0:T(8,128)} %param.6), channel_id=1, source_target_pairs={{0,2},{2,4},{4,6},{6,8},{8,10},{10,12},{12,14},{14,16},{16,18},{18... | collective-permute-start | bytes 6291464 | tf_op jit(solution)/shard_map/ppermute | solution.py:34
  10.4 31.2 %collective-permute-start.1 = (f32[8,65536]{1,0:T(8,128)}, f32[8,65536]{1,0:T(8,128)}, u32[]{:S(2)}, u32[]{:S(2)}) collective-permute-start(f32[8,65536]{1,0:T(8,128)} %param.6), channel_id=1, source_target_pairs={{2,0},{4,2},{6,4},{8,6},{10,8},{12,10},{14,12},{16,14},{18,16},{20... | collective-permute-start | bytes 6291464 | tf_op jit(solution)/shard_map/ppermute | solution.py:37
  14.0 11.4 %collective-permute-start.2 = (bf16[2,1,1,65536]{3,0,2,1:T(2,128)(2,1)S(1)}, bf16[2,1,1,65536]{3,0,2,1:T(2,128)(2,1)S(1)}, u32[]{:S(2)}, u32[]{:S(2)}) collective-permute-start(bf16[2,1,1,65536]{3,0,2,1:T(2,128)(2,1)S(1)} %copy.9), channel_id=1, source_target_pairs={{2,0},{4,2},{6,4},{8,6},{10,8},{12,10},{14,12},{16,14},{18,16},{20... | collective-permute-start | bytes 786440 | tf_op jit(solution)/shard_map/ppermute | solution.py:45
  18.3 1.7 copy-start.5
  18.3 7.7 %collective-permute-start.3 = (bf16[2,1,1,65536]{3,0,2,1:T(2,128)(2,1)}, bf16[2,1,1,65536]{3,0,2,1:T(2,128)(2,1)}, u32[]{:S(2)}, u32[]{:S(2)}) collective-permute-start(bf16[2,1,1,65536]{3,0,2,1:T(2,128)(2,1)} %copy.10), channel_id=1, source_target_pairs={{2,0},{4,2},{6,4},{8,6},{10,8},{12,10},{14,12},{16,14},{18,16},{20... | collective-permute-start | bytes 786440 | tf_op jit(solution)/shard_map/ppermute | solution.py:45
  21.9 2.9 copy-start.9
  24.8 2.8 copy-start.1
  27.6 6.7 %copy-start.6 = (f32[1,65536]{1,0:T(1,128)}, f32[1,65536]{1,0:T(1,128)S(1)}, u32[]{:S(2)}) copy-start(f32[1,65536]{1,0:T(1,128)S(1)} %get-tuple-element.45) | copy-start | bytes 786436
  27.6 6.7 %copy-start.7 = (f32[1,65536]{1,0:T(1,128)}, f32[1,65536]{1,0:T(1,128)S(1)}, u32[]{:S(2)}) copy-start(f32[1,65536]{1,0:T(1,128)S(1)} %get-tuple-element.46) | copy-start | bytes 786436
  27.6 6.6 %copy-start = (f32[8,65536]{1,0:T(8,128)S(1)}, f32[8,65536]{1,0:T(8,128)}, u32[]{:S(2)}) copy-start(f32[8,65536]{1,0:T(8,128)} %get-tuple-element.40) | copy-start | bytes 6291460
  39.1 2.2 copy-start.2
  96.2 70.7 %copy-start.3 = (f32[8,65536]{1,0:T(8,128)S(1)}, f32[8,65536]{1,0:T(8,128)}, u32[]{:S(2)}) copy-start(f32[8,65536]{1,0:T(8,128)} %get-tuple-element.24) | copy-start | bytes 6291460
  96.2 70.7 %copy-start.8 = (pred[8,65536]{1,0:T(8,128)(4,1)S(1)}, pred[8,65536]{1,0:T(8,128)(4,1)}, u32[]{:S(2)}) copy-start(pred[8,65536]{1,0:T(8,128)(4,1)} %get-tuple-element.25) | copy-start | bytes 1572868
  96.2 137.2 %all-gather.2.cloned.1.call-start = ((), (), s32[]{:S(2)}) async-start(), calls=%async_computation.2 | async-start | bytes 3145728 | tf_op jit(solution)/shard_map/all_gather | solution.py:161
  168.7 4.6 %collective-permute-start.5 = (f32[8,32768]{1,0:T(8,128)S(1)}, f32[8,32768]{1,0:T(8,128)S(1)}, u32[]{:S(2)}, u32[]{:S(2)}) collective-permute-start(f32[8,32768]{1,0:T(8,128)S(1)} %fusion.104), channel_id=1, source_target_pairs={{2,0},{4,2},{6,4},{8,6},{10,8},{12,10},{14,12},{16,14},{18,16},{20... | collective-permute-start | bytes 3145736 | tf_op jit(solution)/shard_map/ppermute | solution.py:37
  170.0 5.3 %collective-permute-start.4 = (f32[8,32768]{1,0:T(8,128)S(1)}, f32[8,32768]{1,0:T(8,128)S(1)}, u32[]{:S(2)}, u32[]{:S(2)}) collective-permute-start(f32[8,32768]{1,0:T(8,128)S(1)} %fusion.104), channel_id=1, source_target_pairs={{0,2},{2,4},{4,6},{6,8},{8,10},{10,12},{12,14},{14,16},{16,18},{18... | collective-permute-start | bytes 3145736 | tf_op jit(solution)/shard_map/ppermute | solution.py:34
Sparse Core Ops, SparseCore 0:
  96.3 70.4 reduce-scatter.1
  179.7 53.6 all-gather.1
where the time goes:
time: 301 us; the launch traced here: 300 us
  waiting for transfers between devices  125 us (42%)
  other arithmetic  100 us (33%)
  blocking collectives  33.6 us (11%)
  between operations  15 us (5%)
  local copies, waits for them, and re-layouts  14.1 us (5%)
  starting transfers between devices  12.3 us (4%)
    reduce_scatter x1, waiting for transfers between devices, shards(): share = lax.psum_scatter(local, 'freq', scatter_dimension=1, tiled=True)  69.1 us
    all_gather x1, waiting for transfers between devices, shards(): joined = lax.all_gather(rowed, 'freq', axis=1, tiled=True)  53.8 us
    sub x1, other arithmetic, element_terms(): return stiffness * (elastic - loss_factor * damped) - omega * inertia  46 us
    psum x1, blocking collectives, shards(): total = lax.psum(jnp.sum(back * back), 'rows')  33.6 us
    reduce_sum x1, other arithmetic, shards(): total = lax.psum(jnp.sum(back * back), 'rows')  24.1 us
    concatenate x2, other arithmetic, corners(): stacked = jnp.concatenate([nodes, below], axis=0)  11.5 us
    add x2, other arithmetic, row_pass(): total = total + taps[offset] * padded[offset:offset + count]  11.1 us
    ppermute x2, starting transfers between devices, extended(): lax.ppermute(lax.slice_in_dim(block, block.shape[dim] - width, None, axis...  6.98 us
  transfers between devices with their start and end apart: 8, of which 4 were waited for; matrix products, arithmetic and copies ran while one was open for 9% of the time, Pallas kernels for 0%

commit v1 on v0

v1 whole, which is shorter than its diff:
```python
import functools

import jax
import jax.numpy as jnp
from jax import lax
from jax.experimental import pallas as pl
from jax.experimental.pallas import tpu as pltpu
from jax.sharding import PartitionSpec as P

MESH = pl.DeviceIdType.MESH
RADIUS = 8
SHARP = 8.0
EPSILON = 1e-06
CHUNK = 2048
SUB = 512
LAGS = (2, 2, 2, 2)
BIG = 32767.0


def ds(start, size):
    return pl.ds(pl.multiple_of(start, 128), size)


def wide(tile, width):
    return jnp.concatenate([tile] * (width // tile.shape[1]), axis=1)


def row_taps(low, mid, high):
    row = lax.broadcasted_iota(jnp.int32, mid.shape, 0)
    total = 9.0 * mid + (low + high)
    for s in range(1, 8):
        keep = row >= s
        mixed = float(9 - s) * jnp.where(keep, mid, high) + float(1 + s) * jnp.where(keep, low, mid)
        total = total + pltpu.roll(mixed, 8 - s, 0)
    return total


def col_taps(window):
    width = window.shape[1]

    def ahead(x, k):
        return pltpu.roll(x, width - k, 1)

    def behind(x, k):
        return pltpu.roll(x, k, 1)

    for move in (ahead, behind):
        s = window + move(window, 1)
        s = s + move(s, 2)
        s = s + move(s, 4)
        window = s + move(window, 8)
    return window[:, 128 : width - 128]


def edge_gap(distance):
    gap = jnp.maximum(float(RADIUS) - distance, 0.0)
    return 0.5 * gap * (gap + 1.0)


def peak(blocks):
    acc = None
    for block in blocks:
        for t in range(block.shape[1] // 128):
            tile = jnp.abs(block[:, t * 128 : (t + 1) * 128])
            acc = tile if acc is None else jnp.maximum(acc, tile)
    return acc


def to_code(first, second):
    both = jnp.concatenate([first, second], axis=0)
    return jnp.round(both).astype(jnp.int32).astype(jnp.int16)


def from_code(code):
    both = code.astype(jnp.int32).astype(jnp.float32)
    return both[:8], both[8:]


def kernel(sizes, design_h, passive_h, state_h, adjoint_h, omega_sq, assign, back_o, scale_o, *scratch):
    R, F, N, S = sizes
    C = CHUNK
    half, quarter = C // 2, C // 4
    piece = N // F
    n = piece // C
    L1, L3, L4, L5 = LAGS
    (design, passive, state, adjoint, dq, dlo, dhi, nd, nrecv, nbuf, rowed, tmp, own, factor,
     tq, tsc, trecv, tsr, sq, ssc, slo, slos, shi, shis, gq, gsc, grecv, gsr, joined, part, parts,
     in_sem, d_s, d_r, n_s, n_r, t_s, t_r, s_s, s_r, g_s, g_r, p_s, p_r) = scratch
    r = lax.axis_index("rows")
    me = lax.axis_index("freq")
    has_lo = r > 0
    has_hi = r < R - 1
    below_id = {"rows": jnp.maximum(r - 1, 0)}
    above_id = {"rows": jnp.minimum(r + 1, R - 1)}

    loads = [
        pltpu.make_async_copy(design_h, design, in_sem.at[0]),
        pltpu.make_async_copy(passive_h, passive, in_sem.at[1]),
        pltpu.make_async_copy(state_h, state.at[:, :, :, pl.ds(0, N)], in_sem.at[2]),
        pltpu.make_async_copy(adjoint_h, adjoint.at[:, :, :, pl.ds(0, N)], in_sem.at[3]),
    ]
    for load in loads:
        load.start()

    bar = pltpu.get_barrier_semaphore()
    for d in range(1, R):
        pl.semaphore_signal(bar, inc=1, device_id={"rows": lax.rem(r + d, R)}, device_id_type=MESH)
    for d in range(1, F):
        pl.semaphore_signal(bar, inc=1, device_id={"freq": lax.rem(me + d, F)}, device_id_type=MESH)

    edge = jnp.zeros((8, 128), jnp.float32)
    for buf in (rowed, joined):
        buf[:, pl.ds(0, 128)] = edge
        buf[:, pl.ds(N + 128, 128)] = edge
    for buf in (state, adjoint):
        for j in range(2):
            for s in range(S):
                buf[j, s, :, pl.ds(N, 128)] = edge.astype(jnp.bfloat16)
    nbuf[:, pl.ds(N, 128)] = jnp.zeros((nbuf.shape[0], 128), jnp.float32)

    @pl.when(jnp.logical_not(has_lo))
    def _():
        def fill(g, c):
            dlo[g] = jnp.zeros((16, half), jnp.int16)
            return c

        lax.fori_loop(0, F * n, fill, 0)

        def fill2(g, c):
            slo[g] = jnp.zeros((16, half), jnp.int16)
            slos[g] = edge
            return c

        lax.fori_loop(0, n, fill2, 0)

    @pl.when(jnp.logical_not(has_hi))
    def _():
        def fill(g, c):
            dhi[g] = jnp.zeros((16, half), jnp.int16)
            for s in range(S):
                nrecv[g, s] = jnp.zeros((16, quarter), jnp.bfloat16)
            return c

        lax.fori_loop(0, F * n, fill, 0)

        def fill2(g, c):
            shi[g] = jnp.zeros((16, half), jnp.int16)
            shis[g] = edge
            return c

        lax.fori_loop(0, n, fill2, 0)

    lo_on = has_lo.astype(jnp.float32)
    hi_on = has_hi.astype(jnp.float32)
    row = lax.broadcasted_iota(jnp.int32, (8, 128), 0)
    place = (r * 8 + row).astype(jnp.float32)
    row_inv = 1.0 / (81.0 - edge_gap(place) - edge_gap(float(R * 8 - 1) - place))
    omegas = []
    for s in range(S):
        picked = jnp.float32(0.0)
        for t in range(omega_sq.shape[0]):
            picked = picked + jnp.where(assign[s] == t, omega_sq[t], 0.0)
        omegas.append(picked)

    def remote(src, dst, send, recv, device):
        return pltpu.make_async_remote_copy(
            src_ref=src, dst_ref=dst, send_sem=send, recv_sem=recv, device_id=device, device_id_type=MESH
        )

    def d_up(g):
        return remote(dq.at[g], dlo.at[g], d_s.at[0, g], d_r.at[0, g], above_id)

    def d_down(g):
        return remote(dq.at[g], dhi.at[g], d_s.at[1, g], d_r.at[1, g], below_id)

    def n_down(g):
        return remote(nd.at[g], nrecv.at[g], n_s.at[g], n_r.at[g], below_id)

    def t_copies(d, q):
        to = {"freq": lax.rem(me + d, F)}
        return (
            remote(tq.at[d - 1, q], trecv.at[d - 1, q], t_s.at[0, d - 1, q], t_r.at[0, d - 1, q], to),
            remote(tsc.at[d - 1, q], tsr.at[d - 1, q], t_s.at[1, d - 1, q], t_r.at[1, d - 1, q], to),
        )

    def s_up(q):
        return (
            remote(sq.at[q], slo.at[q], s_s.at[0, q], s_r.at[0, q], above_id),
            remote(ssc.at[q], slos.at[q], s_s.at[1, q], s_r.at[1, q], above_id),
        )

    def s_down(q):
        return (
            remote(sq.at[q], shi.at[q], s_s.at[2, q], s_r.at[2, q], below_id),
            remote(ssc.at[q], shis.at[q], s_s.at[3, q], s_r.at[3, q], below_id),
        )

    def g_copies(d, q):
        to = {"freq": lax.rem(me + d, F)}
        return (
            remote(gq.at[q], grecv.at[d - 1, q], g_s.at[0, d - 1, q], g_r.at[0, d - 1, q], to),
            remote(gsc.at[q], gsr.at[d - 1, q], g_s.at[1, d - 1, q], g_r.at[1, d - 1, q], to),
        )

    def encode(load, code_ref, scale_ref):
        acc = None
        for b in range(C // SUB):
            tile = peak([load(b * SUB, SUB)])
            acc = tile if acc is None else jnp.maximum(acc, tile)
        fine = acc > 1e-30
        scale_ref[...] = jnp.where(fine, acc * (1.0 / BIG), 0.0)
        inv = wide(jnp.where(fine, BIG / jnp.where(fine, acc, 1.0), 0.0), SUB)
        for b in range(half // SUB):
            code_ref[:, pl.ds(b * SUB, SUB)] = to_code(
                load(b * SUB, SUB) * inv, load(half + b * SUB, SUB) * inv
            )

    def stage0(k):
        for p in range(F):
            g = p * n + k
            col = g * C
            for b in range(half // SUB):
                x0 = design[:, ds(col + b * SUB, SUB)]
                x1 = design[:, ds(col + half + b * SUB, SUB)]
                dq[g, :, pl.ds(b * SUB, SUB)] = to_code((x0 - 0.5) * 65536.0, (x1 - 0.5) * 65536.0)
            rows16 = lax.broadcasted_iota(jnp.int32, (8, quarter), 0)
            for s in range(S):
                packs = []
                for src in (state, adjoint):
                    acc = jnp.zeros((8, quarter), jnp.float32)
                    for j in range(2):
                        x = src[j, s, :, ds(col, C)].astype(jnp.float32)[0:1]
                        for b in range(4):
                            line = jnp.broadcast_to(x[:, b * quarter : (b + 1) * quarter], (8, quarter))
                            acc = jnp.where(rows16 == j * 4 + b, line, acc)
                    packs.append(acc)
                nd[g, s] = jnp.concatenate(packs, axis=0).astype(jnp.bfloat16)

    def send0(k):
        for p in range(F):
            g = p * n + k

            @pl.when(has_hi)
            def _():
                d_up(g).start()

            @pl.when(has_lo)
            def _():
                d_down(g).start()
                n_down(g).start()

    def stage1(k):
        for p in range(F):
            g = p * n + k
            col = g * C

            @pl.when(has_lo)
            def _():
                d_up(g).wait_recv()

            @pl.when(has_hi)
            def _():
                d_down(g).wait_recv()
                n_down(g).wait_recv()

            for s in range(S):
                rows16 = nrecv[g, s].astype(jnp.float32)
                for t in range(4):
                    for b in range(4):
                        nbuf[pl.ds(s * 8 + t, 1), ds(col + b * quarter, quarter)] = rows16[
                            t * 4 + b : t * 4 + b + 1
                        ]
            for b in range(half // SUB):
                lows = from_code(dlo[g, :, pl.ds(b * SUB, SUB)])
                highs = from_code(dhi[g, :, pl.ds(b * SUB, SUB)])
                for h in range(2):
                    at = col + h * half + b * SUB
                    low = (lows[h] * (1.0 / 65536.0) + 0.5) * lo_on
                    high = (highs[h] * (1.0 / 65536.0) + 0.5) * hi_on
                    rowed[:, ds(at + 128, SUB)] = row_taps(low, design[:, ds(at, SUB)], high)

    row_sub = lax.broadcasted_iota(jnp.int32, (8, SUB + 128), 0)

    def haar(src, j, s, t, at):
        x = src[j, s, :, ds(at, SUB + 128)].astype(jnp.float32)
        next_line = nbuf[pl.ds(s * 8 + t, 1), ds(at, SUB + 128)]
        below = jnp.where(row_sub == 7, next_line, pltpu.roll(x, 7, 0))
        out = []
        for y in (x + below, x - below):
            right = pltpu.roll(y, SUB + 127, 1)[:, :SUB]
            y = y[:, :SUB]
            out.extend((y + right, y - right))
        return out

    def terms(at):
        j = (at + lax.broadcasted_iota(jnp.int32, (1, SUB), 1)).astype(jnp.float32)
        col_inv = 1.0 / (81.0 - edge_gap(j) - edge_gap(float(N - 1) - j))
        weight = wide(row_inv, SUB) * col_inv
        tilde = col_taps(rowed[:, ds(at, SUB + 256)]) * weight
        top = jnp.tanh(jnp.full((8, SUB), SHARP * 0.5, jnp.float32))
        inv_q = 0.5 / top
        t = jnp.tanh(SHARP * (tilde - 0.5))
        solid = passive[:, ds(at, SUB)] > 0
        density = jnp.where(solid, 1.0, (top + t) * inv_q)
        slope = jnp.where(solid, 0.0, SHARP * (1.0 - t * t) * inv_q)
        stiff = 3.0 * density * density * (1.0 - 0.001)
        total = None
        for s in range(S):
            sr = haar(state, 0, s, 0, at)
            si = haar(state, 1, s, 1, at)
            ar = haar(adjoint, 0, s, 2, at)
            ai = haar(adjoint, 1, s, 3, at)
            direct = [ar[c] * sr[c] - ai[c] * si[c] for c in range(4)]
            cross = [ar[c] * si[c] + ai[c] * sr[c] for c in range(1, 4)]
            mix = [None] + [direct[c] - 0.2 * cross[c - 1] for c in range(1, 4)]
            stiffly = 0.25 * (mix[1] + mix[2]) + (1.0 / 6.0) * mix[3]
            mass = (1.0 / 16.0) * direct[0] + (1.0 / 48.0) * (direct[1] + direct[2]) + (1.0 / 144.0) * direct[3]
            value = stiff * stiffly - omegas[s] * mass
            total = value if total is None else total + value
        return total, slope * weight

    def stage2(q):
        for d in range(1, F):
            col = (lax.rem(me + d, F) * n + q) * C

            def body(b, c):
                value, unused = terms(col + b * SUB)
                tmp[:, ds(b * SUB, SUB)] = value
                return c

            lax.fori_loop(0, C // SUB, body, 0)
            encode(lambda o, w: tmp[:, pl.ds(o, w)], tq.at[d - 1, q], tsc.at[d - 1, q])
        col = (me * n + q) * C

        def body(b, c):
            value, slope = terms(col + b * SUB)
            own[:, ds(q * C + b * SUB, SUB)] = value
            factor[:, ds(q * C + b * SUB, SUB)] = slope
            return c

        lax.fori_loop(0, C // SUB, body, 0)
        for d in range(1, F):
            for copy in t_copies(d, q):
                copy.start()

    def stage3(q):
        for d in range(1, F):
            for copy in t_copies(d, q):
                copy.wait_recv()
        for b in range(half // SUB):
            sums = [own[:, ds(q * C + h * half + b * SUB, SUB)] for h in range(2)]
            for d in range(1, F):
                got = from_code(trecv[d - 1, q, :, pl.ds(b * SUB, SUB)])
                scale = wide(tsr[d - 1, q], SUB)
                sums = [sums[h] + got[h] * scale for h in range(2)]
            for h in range(2):
                at = q * C + h * half + b * SUB
                own[:, ds(at, SUB)] = sums[h] * factor[:, ds(at, SUB)]
        encode(lambda o, w: own[:, ds(q * C + o, w)], sq.at[q], ssc.at[q])

    def send3(q):
        @pl.when(has_hi)
        def _():
            for copy in s_up(q):
                copy.start()

        @pl.when(has_lo)
        def _():
            for copy in s_down(q):
                copy.start()

    def stage4(q):
        @pl.when(has_lo)
        def _():
            for copy in s_up(q):
                copy.wait_recv()

        @pl.when(has_hi)
        def _():
            for copy in s_down(q):
                copy.wait_recv()

        base = (me * n + q) * C + 128
        for b in range(half // SUB):
            lows = from_code(slo[q, :, pl.ds(b * SUB, SUB)])
            highs = from_code(shi[q, :, pl.ds(b * SUB, SUB)])
            los, his = wide(slos[q], SUB), wide(shis[q], SUB)
            for h in range(2):
                at = h * half + b * SUB
                joined[:, ds(base + at, SUB)] = row_taps(
                    lows[h] * los, own[:, ds(q * C + at, SUB)], highs[h] * his
                )
        encode(lambda o, w: joined[:, ds(base + o, w)], gq.at[q], gsc.at[q])

    def send4(q):
        for d in range(1, F):
            for copy in g_copies(d, q):
                copy.start()

    def stage5(q):
        for d in range(1, F):
            for copy in g_copies(d, q):
                copy.wait_recv()
            base = (lax.rem(me + F - d, F) * n + q) * C + 128
            scale = wide(gsr[d - 1, q], SUB)
            for b in range(half // SUB):
                got = from_code(grecv[d - 1, q, :, pl.ds(b * SUB, SUB)])
                for h in range(2):
                    joined[:, ds(base + h * half + b * SUB, SUB)] = got[h] * scale

    for load in loads:
        load.wait()
    pl.semaphore_wait(bar, R - 1 + F - 1)

    o1 = L1
    o2 = o1 + 2
    o3 = o2 + L3
    o4 = o3 + L4
    o5 = o4 + L5

    def guarded(fn, it, offset, turn):
        i = it - offset
        arg = lax.rem(i + 1 + n, n) if turn else i

        @pl.when((i >= 0) & (i < n))
        def _():
            fn(arg)

    def step(it, carry):
        guarded(stage0, it, 0, False)
        guarded(stage3, it, o3, True)
        guarded(send0, it, 0, False)
        guarded(stage4, it, o4, True)
        guarded(send3, it, o3, True)
        guarded(stage1, it, o1, False)
        guarded(send4, it, o4, True)
        guarded(stage2, it, o2, True)
        guarded(stage5, it, o5, True)
        return carry

    lax.fori_loop(0, n + o5, step, 0)

    def last(b, acc):
        at = b * SUB
        value = col_taps(joined[:, ds(at, SUB + 256)])
        back_o[:, ds(at, SUB)] = value
        for t in range(SUB // 128):
            tile = value[:, t * 128 : (t + 1) * 128]
            acc = acc + tile * tile
        return acc

    part[...] = lax.fori_loop(0, N // SUB, last, edge)

    def send_waits(k, c):
        for p in range(F):
            g = p * n + k

            @pl.when(has_hi)
            def _():
                d_up(g).wait_send()

            @pl.when(has_lo)
            def _():
                d_down(g).wait_send()
                n_down(g).wait_send()

        for d in range(1, F):
            for copy in t_copies(d, k) + g_copies(d, k):
                copy.wait_send()

        @pl.when(has_hi)
        def _():
            for copy in s_up(k):
                copy.wait_send()

        @pl.when(has_lo)
        def _():
            for copy in s_down(k):
                copy.wait_send()

        return c

    lax.fori_loop(0, n, send_waits, 0)

    def sum_copy(d):
        return remote(part, parts.at[d - 1], p_s.at[d - 1], p_r.at[d - 1], {"rows": lax.rem(r + d, R)})

    for d in range(1, R):
        sum_copy(d).start()
    acc = part[...]
    for d in range(1, R):
        sum_copy(d).wait_recv()
        acc = acc + parts[d - 1]
    total = jnp.sum(acc, keepdims=True)
    scale_o[...] = jnp.broadcast_to(lax.rsqrt(total / float(R * 8 * N) + EPSILON), (8, 128))
    for d in range(1, R):
        sum_copy(d).wait_send()


def shards(sizes, design, passive, state, adjoint, omega_sq, assign):
    R, F, N, S = sizes
    C = CHUNK
    half, quarter = C // 2, C // 4
    piece = N // F
    n = piece // C
    G = F * n
    f32, i16, bf16 = jnp.float32, jnp.int16, jnp.bfloat16
    V = pltpu.VMEM
    dma = pltpu.SemaphoreType.DMA
    scratch = [
        V((8, N), f32), V((8, N), jnp.int32), V((2, S, 8, N + 128), bf16), V((2, S, 8, N + 128), bf16),
        V((G, 16, half), i16), V((G, 16, half), i16), V((G, 16, half), i16),
        V((G, S, 16, quarter), bf16), V((G, S, 16, quarter), bf16), V((8 * S, N + 128), f32),
        V((8, N + 256), f32), V((8, C), f32), V((8, piece), f32), V((8, piece), f32),
        V((F - 1, n, 16, half), i16), V((F - 1, n, 8, 128), f32),
        V((F - 1, n, 16, half), i16), V((F - 1, n, 8, 128), f32),
        V((n, 16, half), i16), V((n, 8, 128), f32),
        V((n, 16, half), i16), V((n, 8, 128), f32), V((n, 16, half), i16), V((n, 8, 128), f32),
        V((n, 16, half), i16), V((n, 8, 128), f32),
        V((F - 1, n, 16, half), i16), V((F - 1, n, 8, 128), f32),
        V((8, N + 256), f32), V((8, 128), f32), V((R - 1, 8, 128), f32),
        dma((4,)), dma((2, G)), dma((2, G)), dma((G,)), dma((G,)),
        dma((2, F - 1, n)), dma((2, F - 1, n)), dma((4, n)), dma((4, n)),
        dma((2, F - 1, n)), dma((2, F - 1, n)), dma((R - 1,)), dma((R - 1,)),
    ]
    anywhere = pl.BlockSpec(memory_space=pl.ANY)
    small = pl.BlockSpec(memory_space=pltpu.SMEM)
    vmem = pl.BlockSpec(memory_space=pltpu.VMEM)
    back, scale = pl.pallas_call(
        functools.partial(kernel, sizes),
        out_shape=(jax.ShapeDtypeStruct((8, N), f32), jax.ShapeDtypeStruct((8, 128), f32)),
        in_specs=[anywhere] * 4 + [small] * 2,
        out_specs=(vmem, vmem),
        scratch_shapes=scratch,
        compiler_params=pltpu.CompilerParams(
            collective_id=0, has_side_effects=True, vmem_limit_bytes=60 * 1024 * 1024
        ),
    )(design, passive, state, adjoint, omega_sq, assign)
    return back * scale[:1, :1]


def solution(mesh):
    R, F = mesh.shape["rows"], mesh.shape["freq"]

    def run(design, passive, state, adjoint, omega_sq, assign):
        sizes = (R, F, design.shape[1], state.shape[1])
        return shards(sizes, design, passive, state, adjoint, omega_sq, assign)

    return jax.shard_map(
        run,
        mesh=mesh,
        in_specs=(
            P("rows", None),
            P("rows", None),
            P(None, "freq", "rows", None),
            P(None, "freq", "rows", None),
            P(),
            P("freq"),
        ),
        out_specs=P("rows", None),
        check_vma=False,
    )
```

time: 301 us -> 164 us (0.54)
  Pallas kernels: 0 us -> 158 us
  waiting for transfers between devices: 125 us -> 0 us
  other arithmetic: 100 us -> 3.66 us
  blocking collectives: 33.6 us -> 0 us
  between operations: 15 us -> 0.66 us
  local copies, waits for them, and re-layouts: 14.1 us -> 1.19 us
  starting transfers between devices: 12.3 us -> 0 us
    pallas_call x0 -> x1, Pallas kernels: none -> 158 us  [shards(): pl.pallas_call(functools.partial(kernel, sizes), out_shape=(jax.ShapeDtyp...]
    reduce_scatter x1 -> x0, waiting for transfers between devices: 69.1 us -> none  [shards(): share = lax.psum_scatter(local, 'freq', scatter_dimension=1, tiled=True)]
    all_gather x1 -> x0, waiting for transfers between devices: 53.8 us -> none  [shards(): joined = lax.all_gather(rowed, 'freq', axis=1, tiled=True)]
    sub x1 -> x0, other arithmetic: 46 us -> none  [element_terms(): return stiffness * (elastic - loss_factor * damped) - omega * inertia]
    psum x1 -> x0, blocking collectives: 33.6 us -> none  [shards(): total = lax.psum(jnp.sum(back * back), 'rows')]
    reduce_sum x2 -> x0, other arithmetic: 24.7 us -> none  [the longest x1 24.1 us: shards(): total = lax.psum(jnp.sum(back * back), 'rows')]
    ppermute x6 -> x0, starting transfers between devices: 12.3 us -> none  [the longest x2 6.98 us: extended(): lax.ppermute(lax.slice_in_dim(block, block.shape[dim] - width, None, axis...]
    concatenate x2 -> x0, other arithmetic: 11.5 us -> none  [corners(): stacked = jnp.concatenate([nodes, below], axis=0)]
  transfers between devices with their start and end apart: 8 -> 0, of which waited for: 4 -> 0; matrix products, arithmetic and copies ran while one was open for 9% -> 0% of each run, Pallas kernels for 0% -> 0%
where the time goes in v1:
time: 164 us; the launch traced here: 163 us
  Pallas kernels  158 us (96%)
  other arithmetic  3.66 us (2%)
    pallas_call x1, Pallas kernels, shards(): pl.pallas_call(functools.partial(kernel, sizes), out_shape=(jax.ShapeDtyp...  158 us
    mul x1, other arithmetic, shards(): return back * scale[:1, :1]  3.66 us

profile of v1, /device:TPU:0, one launch (start us, length us, event | category | flops | bytes accessed | tf_op | source)
XLA Modules:
  0.0 163.5 jit_solution(12736407928153059668)
XLA Ops:
  0.7 158.0 %shard_map.64 = (f32[8,65536]{1,0:T(8,128)}, f32[8,128]{1,0:T(8,128)}) custom-call(f32[8,65536]{1,0:T(8,128)} %design_h.1, s32[8,65536]{1,0:T(8,128)} %passive_h.1, bf16[2,1,8,65536]{3,2,1,0:T(8,128)(2,1)} %state_h.1, bf16[2,1,8,65536]{3,2,1,0:T(8,128)(2,1)} %adjoint_h.1, f32[2]{0:T(128)} %omega_sq.1, s32[1]{0:T(128)S(6)} %copy.7.assign), custom_call_target="tpu_custom_call" | custom-call | tf_op jit(solution)/shard_map/pallas_call | solution.py:529
  158.6 1.2 slice.3
  159.8 3.7 %broadcast_multiply_fusion = f32[8,65536]{1,0:T(8,128)} fusion(f32[8,65536]{1,0:T(8,128)} %get-tuple-element.7, f32[]{:T(128)} %bitcast), kind=kLoop, calls=%fused_computation | loop fusion | flops 524288 | bytes 4194308 | tf_op jit(solution)/shard_map/mul | solution.py:539

commit v2 on v1

--- a/solution.py
+++ b/solution.py
@@ -13,6 +13,11 @@
 EPSILON = 1e-06
 CHUNK = 2048
 SUB = 512
+CSUB = 1024
+TSUB = 512
+TUN = 4
+CUN = 2
+LUN = 4
 LAGS = (2, 2, 2, 2)
 BIG = 32767.0
 
@@ -83,7 +88,7 @@
     piece = N // F
     n = piece // C
     L1, L3, L4, L5 = LAGS
-    (design, passive, state, adjoint, dq, dlo, dhi, nd, nrecv, nbuf, rowed, tmp, own, factor,
+    (design, passive, state, adjoint, dq, dlo, dhi, nd, nrecv, nbuf, rowed, tmp, filt, own, factor,
      tq, tsc, trecv, tsr, sq, ssc, slo, slos, shi, shis, gq, gsc, grecv, gsr, joined, part, parts,
      in_sem, d_s, d_r, n_s, n_r, t_s, t_r, s_s, s_r, g_s, g_r, p_s, p_r) = scratch
     r = lax.axis_index("rows")
@@ -279,28 +284,28 @@
                     high = (highs[h] * (1.0 / 65536.0) + 0.5) * hi_on
                     rowed[:, ds(at + 128, SUB)] = row_taps(low, design[:, ds(at, SUB)], high)
 
-    row_sub = lax.broadcasted_iota(jnp.int32, (8, SUB + 128), 0)
+    row_sub = lax.broadcasted_iota(jnp.int32, (8, TSUB + 128), 0)
 
     def haar(src, j, s, t, at):
-        x = src[j, s, :, ds(at, SUB + 128)].astype(jnp.float32)
-        next_line = nbuf[pl.ds(s * 8 + t, 1), ds(at, SUB + 128)]
+        x = src[j, s, :, ds(at, TSUB + 128)].astype(jnp.float32)
+        next_line = nbuf[pl.ds(s * 8 + t, 1), ds(at, TSUB + 128)]
         below = jnp.where(row_sub == 7, next_line, pltpu.roll(x, 7, 0))
         out = []
         for y in (x + below, x - below):
-            right = pltpu.roll(y, SUB + 127, 1)[:, :SUB]
-            y = y[:, :SUB]
+            right = pltpu.roll(y, TSUB + 127, 1)[:, :TSUB]
+            y = y[:, :TSUB]
             out.extend((y + right, y - right))
         return out
 
-    def terms(at):
-        j = (at + lax.broadcasted_iota(jnp.int32, (1, SUB), 1)).astype(jnp.float32)
+    def terms(at, o):
+        j = (at + lax.broadcasted_iota(jnp.int32, (1, TSUB), 1)).astype(jnp.float32)
         col_inv = 1.0 / (81.0 - edge_gap(j) - edge_gap(float(N - 1) - j))
-        weight = wide(row_inv, SUB) * col_inv
-        tilde = col_taps(rowed[:, ds(at, SUB + 256)]) * weight
-        top = jnp.tanh(jnp.full((8, SUB), SHARP * 0.5, jnp.float32))
+        weight = wide(row_inv, TSUB) * col_inv
+        tilde = filt[:, ds(o, TSUB)] * weight
+        top = jnp.tanh(jnp.full((8, TSUB), SHARP * 0.5, jnp.float32))
         inv_q = 0.5 / top
         t = jnp.tanh(SHARP * (tilde - 0.5))
-        solid = passive[:, ds(at, SUB)] > 0
+        solid = passive[:, ds(at, TSUB)] > 0
         density = jnp.where(solid, 1.0, (top + t) * inv_q)
         slope = jnp.where(solid, 0.0, SHARP * (1.0 - t * t) * inv_q)
         stiff = 3.0 * density * density * (1.0 - 0.001)
@@ -319,26 +324,37 @@
             total = value if total is None else total + value
         return total, slope * weight
 
+    def filtered(col):
+        def body(b, c):
+            filt[:, ds(b * CSUB, CSUB)] = col_taps(rowed[:, ds(col + b * CSUB, CSUB + 256)])
+            return c
+
+        lax.fori_loop(0, C // CSUB, body, 0, unroll=CUN)
+
     def stage2(q):
         for d in range(1, F):
             col = (lax.rem(me + d, F) * n + q) * C
 
+            filtered(col)
+
             def body(b, c):
-                value, unused = terms(col + b * SUB)
-                tmp[:, ds(b * SUB, SUB)] = value
+                value, unused = terms(col + b * TSUB, b * TSUB)
+                tmp[:, ds(b * TSUB, TSUB)] = value
                 return c
 
-            lax.fori_loop(0, C // SUB, body, 0)
+            lax.fori_loop(0, C // TSUB, body, 0, unroll=TUN)
             encode(lambda o, w: tmp[:, pl.ds(o, w)], tq.at[d - 1, q], tsc.at[d - 1, q])
         col = (me * n + q) * C
 
+        filtered(col)
+
         def body(b, c):
-            value, slope = terms(col + b * SUB)
-            own[:, ds(q * C + b * SUB, SUB)] = value
-            factor[:, ds(q * C + b * SUB, SUB)] = slope
+            value, slope = terms(col + b * TSUB, b * TSUB)
+            own[:, ds(q * C + b * TSUB, TSUB)] = value
+            factor[:, ds(q * C + b * TSUB, TSUB)] = slope
             return c
 
-        lax.fori_loop(0, C // SUB, body, 0)
+        lax.fori_loop(0, C // TSUB, body, 0, unroll=TUN)
         for d in range(1, F):
             for copy in t_copies(d, q):
                 copy.start()
@@ -441,15 +457,15 @@
     lax.fori_loop(0, n + o5, step, 0)
 
     def last(b, acc):
-        at = b * SUB
-        value = col_taps(joined[:, ds(at, SUB + 256)])
-        back_o[:, ds(at, SUB)] = value
-        for t in range(SUB // 128):
+        at = b * CSUB
+        value = col_taps(joined[:, ds(at, CSUB + 256)])
+        back_o[:, ds(at, CSUB)] = value
+        for t in range(CSUB // 128):
             tile = value[:, t * 128 : (t + 1) * 128]
             acc = acc + tile * tile
         return acc
 
-    part[...] = lax.fori_loop(0, N // SUB, last, edge)
+    part[...] = lax.fori_loop(0, N // CSUB, last, edge, unroll=LUN)
 
     def send_waits(k, c):
         for p in range(F):
@@ -511,7 +527,7 @@
         V((8, N), f32), V((8, N), jnp.int32), V((2, S, 8, N + 128), bf16), V((2, S, 8, N + 128), bf16),
         V((G, 16, half), i16), V((G, 16, half), i16), V((G, 16, half), i16),
         V((G, S, 16, quarter), bf16), V((G, S, 16, quarter), bf16), V((8 * S, N + 128), f32),
-        V((8, N + 256), f32), V((8, C), f32), V((8, piece), f32), V((8, piece), f32),
+        V((8, N + 256), f32), V((8, C), f32), V((8, C), f32), V((8, piece), f32), V((8, piece), f32),
         V((F - 1, n, 16, half), i16), V((F - 1, n, 8, 128), f32),
         V((F - 1, n, 16, half), i16), V((F - 1, n, 8, 128), f32),
         V((n, 16, half), i16), V((n, 8, 128), f32),

time: 164 us -> 86.7 us (0.53)
  Pallas kernels: 158 us -> 81 us
    pallas_call x1, Pallas kernels: 158 us -> 81 us  [shards(): pl.pallas_call(functools.partial(kernel, sizes), out_shape=(jax.ShapeDtyp...]
where the time goes in v2:
time: 86.7 us; the launch traced here: 86.5 us
  Pallas kernels  81 us (93%)
  other arithmetic  3.66 us (4%)
  local copies, waits for them, and re-layouts  1.19 us (1%)
    pallas_call x1, Pallas kernels, shards(): pl.pallas_call(functools.partial(kernel, sizes), out_shape=(jax.ShapeDtyp...  81 us
    mul x1, other arithmetic, shards(): return back * scale[:1, :1]  3.66 us

profile of v2, /device:TPU:0, one launch (start us, length us, event | category | flops | bytes accessed | tf_op | source)
XLA Modules:
  0.0 86.5 jit_solution(14894201386122796435)
XLA Ops:
  0.7 81.0 %shard_map.64 = (f32[8,65536]{1,0:T(8,128)}, f32[8,128]{1,0:T(8,128)}) custom-call(f32[8,65536]{1,0:T(8,128)} %design_h.1, s32[8,65536]{1,0:T(8,128)} %passive_h.1, bf16[2,1,8,65536]{3,2,1,0:T(8,128)(2,1)} %state_h.1, bf16[2,1,8,65536]{3,2,1,0:T(8,128)(2,1)} %adjoint_h.1, f32[2]{0:T(128)} %omega_sq.1, s32[1]{0:T(128)S(6)} %copy.7.assign), custom_call_target="tpu_custom_call" | custom-call | tf_op jit(solution)/shard_map/pallas_call | solution.py:545
  81.7 1.2 %slice.3 = f32[1,1]{1,0:T(1,128)} slice(f32[8,128]{1,0:T(8,128)} %get-tuple-element.8), slice={[0:1], [0:1]} | slice | bytes 8 | tf_op jit(solution)/shard_map/slice | solution.py:555
  82.9 3.7 %broadcast_multiply_fusion = f32[8,65536]{1,0:T(8,128)} fusion(f32[8,65536]{1,0:T(8,128)} %get-tuple-element.7, f32[]{:T(128)} %bitcast), kind=kLoop, calls=%fused_computation | loop fusion | flops 524288 | bytes 4194308 | tf_op jit(solution)/shard_map/mul | solution.py:555

commit v3 on v2

--- a/solution.py
+++ b/solution.py
@@ -13,12 +13,11 @@
 EPSILON = 1e-06
 CHUNK = 2048
 SUB = 512
-CSUB = 1024
+CSUB = 2048
 TSUB = 512
 TUN = 4
-CUN = 2
-LUN = 4
-LAGS = (2, 2, 2, 2)
+CUN = 1
+LAGS = (2, 3, 2, 2)
 BIG = 32767.0
 
 
@@ -98,14 +97,25 @@
     below_id = {"rows": jnp.maximum(r - 1, 0)}
     above_id = {"rows": jnp.minimum(r + 1, R - 1)}
 
-    loads = [
-        pltpu.make_async_copy(design_h, design, in_sem.at[0]),
-        pltpu.make_async_copy(passive_h, passive, in_sem.at[1]),
-        pltpu.make_async_copy(state_h, state.at[:, :, :, pl.ds(0, N)], in_sem.at[2]),
-        pltpu.make_async_copy(adjoint_h, adjoint.at[:, :, :, pl.ds(0, N)], in_sem.at[3]),
-    ]
-    for load in loads:
-        load.start()
+    def loads(k):
+        copies = []
+        for p in range(F):
+            g = p * n + k
+            cols = ds(g * C, C)
+            copies += [
+                pltpu.make_async_copy(design_h.at[:, cols], design.at[:, cols], in_sem.at[0, g]),
+                pltpu.make_async_copy(state_h.at[:, :, :, cols], state.at[:, :, :, cols], in_sem.at[1, g]),
+                pltpu.make_async_copy(adjoint_h.at[:, :, :, cols], adjoint.at[:, :, :, cols], in_sem.at[2, g]),
+                pltpu.make_async_copy(passive_h.at[:, cols], passive.at[:, cols], in_sem.at[3, g]),
+            ]
+        return copies
+
+    def begin(k, c):
+        for copy in loads(k):
+            copy.start()
+        return c
+
+    lax.fori_loop(0, n, begin, 0)
 
     bar = pltpu.get_barrier_semaphore()
     for d in range(1, R):
@@ -221,6 +231,8 @@
             )
 
     def stage0(k):
+        for copy in loads(k):
+            copy.wait()
         for p in range(F):
             g = p * n + k
             col = g * C
@@ -424,8 +436,22 @@
                 for h in range(2):
                     joined[:, ds(base + h * half + b * SUB, SUB)] = got[h] * scale
 
-    for load in loads:
-        load.wait()
+    def stage6(q):
+        for p in range(F):
+            col = (p * n + q) * C
+
+            def body(b, acc):
+                at = col + b * CSUB
+                value = col_taps(joined[:, ds(at, CSUB + 256)])
+                back_o[:, ds(at, CSUB)] = value
+                for t in range(CSUB // 128):
+                    tile = value[:, t * 128 : (t + 1) * 128]
+                    acc = acc + tile * tile
+                return acc
+
+            part[...] = lax.fori_loop(0, C // CSUB, body, part[...], unroll=CUN)
+
+    part[...] = edge
     pl.semaphore_wait(bar, R - 1 + F - 1)
 
     o1 = L1
@@ -433,39 +459,30 @@
     o3 = o2 + L3
     o4 = o3 + L4
     o5 = o4 + L5
+    o6 = o5 + 2
 
     def guarded(fn, it, offset, turn):
         i = it - offset
-        arg = lax.rem(i + 1 + n, n) if turn else i
+        arg = lax.rem(i + turn + n, n)
 
         @pl.when((i >= 0) & (i < n))
         def _():
             fn(arg)
 
     def step(it, carry):
-        guarded(stage0, it, 0, False)
-        guarded(stage3, it, o3, True)
-        guarded(send0, it, 0, False)
-        guarded(stage4, it, o4, True)
-        guarded(send3, it, o3, True)
-        guarded(stage1, it, o1, False)
-        guarded(send4, it, o4, True)
-        guarded(stage2, it, o2, True)
-        guarded(stage5, it, o5, True)
+        guarded(stage0, it, 0, 0)
+        guarded(stage3, it, o3, 1)
+        guarded(send0, it, 0, 0)
+        guarded(stage4, it, o4, 1)
+        guarded(send3, it, o3, 1)
+        guarded(stage1, it, o1, 0)
+        guarded(send4, it, o4, 1)
+        guarded(stage2, it, o2, 1)
+        guarded(stage5, it, o5, 1)
+        guarded(stage6, it, o6, 2)
         return carry
 
-    lax.fori_loop(0, n + o5, step, 0)
-
-    def last(b, acc):
-        at = b * CSUB
-        value = col_taps(joined[:, ds(at, CSUB + 256)])
-        back_o[:, ds(at, CSUB)] = value
-        for t in range(CSUB // 128):
-            tile = value[:, t * 128 : (t + 1) * 128]
-            acc = acc + tile * tile
-        return acc
-
-    part[...] = lax.fori_loop(0, N // CSUB, last, edge, unroll=LUN)
+    lax.fori_loop(0, n + o6, step, 0)
 
     def send_waits(k, c):
         for p in range(F):
@@ -508,7 +525,8 @@
         sum_copy(d).wait_recv()
         acc = acc + parts[d - 1]
     total = jnp.sum(acc, keepdims=True)
-    scale_o[...] = jnp.broadcast_to(lax.rsqrt(total / float(R * 8 * N) + EPSILON), (8, 128))
+    inverse = lax.rsqrt(jnp.broadcast_to(total, (8, 128)) / float(R * 8 * N) + EPSILON)
+    scale_o[0, 0] = jnp.max(inverse)
     for d in range(1, R):
         sum_copy(d).wait_send()
 
@@ -535,7 +553,7 @@
         V((n, 16, half), i16), V((n, 8, 128), f32),
         V((F - 1, n, 16, half), i16), V((F - 1, n, 8, 128), f32),
         V((8, N + 256), f32), V((8, 128), f32), V((R - 1, 8, 128), f32),
-        dma((4,)), dma((2, G)), dma((2, G)), dma((G,)), dma((G,)),
+        dma((4, G)), dma((2, G)), dma((2, G)), dma((G,)), dma((G,)),
         dma((2, F - 1, n)), dma((2, F - 1, n)), dma((4, n)), dma((4, n)),
         dma((2, F - 1, n)), dma((2, F - 1, n)), dma((R - 1,)), dma((R - 1,)),
     ]
@@ -544,15 +562,15 @@
     vmem = pl.BlockSpec(memory_space=pltpu.VMEM)
     back, scale = pl.pallas_call(
         functools.partial(kernel, sizes),
-        out_shape=(jax.ShapeDtypeStruct((8, N), f32), jax.ShapeDtypeStruct((8, 128), f32)),
+        out_shape=(jax.ShapeDtypeStruct((8, N), f32), jax.ShapeDtypeStruct((1, 1), f32)),
         in_specs=[anywhere] * 4 + [small] * 2,
-        out_specs=(vmem, vmem),
+        out_specs=(vmem, small),
         scratch_shapes=scratch,
         compiler_params=pltpu.CompilerParams(
             collective_id=0, has_side_effects=True, vmem_limit_bytes=60 * 1024 * 1024
         ),
     )(design, passive, state, adjoint, omega_sq, assign)
-    return back * scale[:1, :1]
+    return back * scale
 
 
 def solution(mesh):

time: 86.7 us -> 80 us (0.923)
  Pallas kernels: 81 us -> 75.5 us
  local copies, waits for them, and re-layouts: 1.19 us -> 0 us
    pallas_call x1, Pallas kernels: 81 us -> 75.5 us  [shards(): pl.pallas_call(functools.partial(kernel, sizes), out_shape=(jax.ShapeDtyp...]
    slice x1 -> x0, local copies, waits for them, and re-layouts: 1.19 us -> none  [shards(): return back * scale[:1, :1]]
where the time goes in v3:
time: 80 us; the launch traced here: 79.8 us
  Pallas kernels  75.5 us (94%)
  other arithmetic  3.65 us (5%)
    pallas_call x1, Pallas kernels, shards(): pl.pallas_call(functools.partial(kernel, sizes), out_shape=(jax.ShapeDtyp...  75.5 us
    mul x1, other arithmetic, shards(): return back * scale  3.65 us

profile of v3, /device:TPU:0, one launch (start us, length us, event | category | flops | bytes accessed | tf_op | source)
XLA Modules:
  0.0 79.8 jit_solution(5598218974968622490)
XLA Ops:
  0.7 75.5 %shard_map.64 = (f32[8,65536]{1,0:T(8,128)}, f32[1,1]{1,0:T(1,128)}) custom-call(f32[8,65536]{1,0:T(8,128)} %design_h.1, s32[8,65536]{1,0:T(8,128)} %passive_h.1, bf16[2,1,8,65536]{3,2,1,0:T(8,128)(2,1)} %state_h.1, bf16[2,1,8,65536]{3,2,1,0:T(8,128)(2,1)} %adjoint_h.1, f32[2]{0:T(128)} %omega_sq.1, s32[1]{0:T(128)S(6)} %copy.7.assign), custom_call_target="tpu_custom_call" | custom-call | tf_op jit(solution)/shard_map/pallas_call | solution.py:563
  76.2 3.7 %broadcast_multiply_fusion = f32[8,65536]{1,0:T(8,128)} fusion(f32[8,65536]{1,0:T(8,128)} %get-tuple-element.7, f32[]{:T(128)} %bitcast), kind=kLoop, calls=%fused_computation | loop fusion | flops 524288 | bytes 4194308 | tf_op jit(solution)/shard_map/mul | solution.py:573
